TPU v7x, 256 devices: a whole 4x4x8 slice. The times are simulated.
256 devices in a mesh: trow: 4 (over y), tcol: 4 (over x), pix: 16 (over z, core).
Axes of the slice: x: 4, y: 4, z: 8, core: 2. Of those that a mesh axis runs over, the one named last changes fastest.
Arguments:
- frames: float32 [6144, 2, 64, 128], P(('trow', 'tcol'), None, 'pix'), may hold values from 0.1 to 8
- drift: int32 [6144, 2], P(('trow', 'tcol')), may hold values from -7 to 7
Outputs:
- inner_cycle: float32 [6144, 6144], P(('trow', 'pix'), 'tcol')
- second_band_twotime: float32 [6144, 6144], P(('trow', 'pix'), 'tcol')
All inputs are finite; a program needn't handle non-finite values.
Results may differ from a plain program's by a relative error of at most 0.0003.
Values may be sent and summed in bfloat16 or wider, within the bound.
A program may use at most 128 MiB of HBM per device.

v0:
```python
import jax
import jax.numpy as jnp
from jax import lax
from jax.sharding import PartitionSpec as P


def extended(cells, sides, width):
    for axis, dim in sides:
        count = lax.axis_size(axis)
        ends = count - 1
        head = lax.slice_in_dim(cells, 0, width, axis=dim)
        tail = lax.slice_in_dim(cells, cells.shape[dim] - width, cells.shape[dim], axis=dim)
        cells = jnp.concatenate(
            [
                lax.ppermute(tail, axis, [(i, (i + 1) % count) for i in range(ends)]),
                cells,
                lax.ppermute(head, axis, [((i + 1) % count, i) for i in range(ends)]),
            ],
            axis=dim,
        )
    return cells


def blend(padded, steps, device_axis):
    upward = (jnp.maximum(steps, 0).astype(jnp.float32) / 8.0)[:, None, None, None]
    downward = (jnp.maximum(-steps, 0).astype(jnp.float32) / 8.0)[:, None, None, None]
    length = padded.shape[device_axis] - 2
    middle = lax.slice_in_dim(padded, 1, 1 + length, 1, device_axis)
    after = lax.slice_in_dim(padded, 2, 2 + length, 1, device_axis)
    before = lax.slice_in_dim(padded, 0, length, 1, device_axis)
    return (1.0 - upward - downward) * middle + upward * after + downward * before


def per_device(frames, drift):
    local_frames = frames.shape[0]
    tile_rows = frames.shape[2]
    columns = frames.shape[3]
    total_frames = local_frames * lax.axis_size("trow") * lax.axis_size("tcol")
    band_pixels = tile_rows * columns * lax.axis_size("pix")
    padded = extended(frames.astype(jnp.bfloat16), (("pix", 2),), 1).astype(frames.dtype)
    rowpass = blend(padded, drift[:, 0], 2)
    padded = jnp.pad(rowpass, ((0, 0), (0, 0), (0, 0), (1, 1)))
    shifted = blend(padded, drift[:, 1], 3)
    pixel_mean = lax.psum(jnp.sum(shifted, axis=0), ("trow", "tcol")) / total_frames
    flat = shifted / pixel_mean[None]
    frame_mean = lax.psum(jnp.sum(flat, axis=(2, 3)), "pix") / band_pixels
    normed = (flat / frame_mean[:, :, None, None]).astype(jnp.bfloat16)
    normed = normed.reshape(local_frames, 2, tile_rows * columns)
    block_size = local_frames * lax.axis_size("tcol")
    everything = lax.all_gather(normed, ("trow", "tcol"), axis=0, tiled=True)
    row_frames = lax.dynamic_slice_in_dim(
        everything, lax.axis_index("trow") * block_size, block_size, 0
    )
    col_frames = lax.dynamic_slice_in_dim(
        everything, lax.axis_index("tcol") * block_size, block_size, 0
    )
    own_rows = block_size // lax.axis_size("pix")
    results = []
    for band in range(2):
        band_rows = row_frames[:, band]
        band_cols = col_frames[:, band]

        def partial_gram(start, count, band_rows=band_rows, band_cols=band_cols):
            return lax.dot_general(
                band_rows, band_cols, (((1,), (1,)), ((), ())), preferred_element_type=jnp.float32
            )

        summed = lax.psum_scatter(
            partial_gram(jnp.int32(0), lax.axis_size("pix") * own_rows),
            "pix",
            scatter_dimension=0,
            tiled=True,
        )
        results.append(summed / band_pixels)
    return (results[0], results[1])


def solution(mesh):
    in_specs = (P(("trow", "tcol"), None, "pix", None), P(("trow", "tcol"), None))
    out_specs = (P(("trow", "pix"), "tcol"), P(("trow", "pix"), "tcol"))
    return jax.shard_map(
        per_device, mesh=mesh, in_specs=in_specs, out_specs=out_specs, check_vma=False
    )
```

profile of v0, /device:TPU:8, one launch (start us, length us, event | category | flops | bytes accessed | tf_op | source)
XLA Modules:
  0.0 343.0 jit_solution(5031230959455782191)
XLA Ops:
  7.2 0.0 all-gather.2.cloned.1.call-start
  7.2 1.7 copy.10
  9.0 1.8 collective-permute-start
  10.7 1.3 collective-permute-start.1
  12.1 3.7 %collective-permute-done.1 = bf16[384,2,1,128]{3,0,2,1:T(8,128)(2,1)S(1)} collective-permute-done((bf16[384,2,1,128]{3,0,2,1:T(8,128)(2,1)S(1)}, bf16[384,2,1,128]{3,0,2,1:T(8,128)(2,1)S(1)}, u32[]{:S(2)}, u32[]{:S(2)}) %collective-permute-start.1) | collective-permute-done | bytes 196640 | tf_op jit(solution)/shard_map/ppermute | solution.py:17
  15.8 0.2 maximum_convert_fusion
  15.9 0.4 fusion.6
  16.3 1.0 fusion.11
  17.4 34.5 %psum.14 = f32[2,4,128]{2,1,0:T(4,128)S(1)} all-reduce(f32[2,4,128]{2,1,0:T(4,128)S(1)} %get-tuple-element.6), channel_id=1, replica_groups=mesh['trow'=4,'tcol'=4,'pix'=16] {'trow','tcol'}, use_global_device_ids=true, to_apply=%region_1.2 | all-reduce | flops 1024 | bytes 8192 | tf_op jit(solution)/shard_map/psum | solution.py:44
  51.9 0.2 divide_reduce_fusion
  52.1 28.0 %psum.15 = f32[384,2]{0,1:T(2,128)S(1)} all-reduce(f32[384,2]{0,1:T(2,128)S(1)} %divide_reduce_fusion), channel_id=1, replica_groups=mesh['trow'=4,'tcol'=4,'pix'=16] {'pix'}, use_global_device_ids=true, to_apply=%region_3.4 | all-reduce | flops 768 | bytes 6144 | tf_op jit(solution)/shard_map/psum | solution.py:46
  80.1 1.2 copy_bitcast_fusion
  81.3 0.0 all-gather.2.cloned.1.call-update
  81.4 0.0 reduce-scatter.5.cloned.1.call-start
  81.4 97.7 %all-gather.2.cloned.1.call-done = bf16[6144,2,512]{2,0,1:T(8,128)(2,1)} async-done(((bf16[384,2,512]{2,0,1:T(8,128)(2,1)}), bf16[6144,2,512]{2,0,1:T(8,128)(2,1)}) %all-gather.2.cloned.1.call-update) | async-done | bytes 12582928 | tf_op jit(solution)/shard_map/all_gather | solution.py:50
  179.1 8.2 %fusion.4 = f32[1536,1536]{1,0:T(8,128)} fusion(bf16[6144,2,512]{2,0,1:T(8,128)(2,1)} %all-gather.2.cloned.1.call-done, s32[]{:T(128)S(6)} %select_n.7, s32[]{:T(128)S(6)} %add.38, s32[]{:T(128)S(6)} %select_n.6), kind=kOutput, calls=%fused_computation.7 | convolution fusion | flops 2415919104 | bytes 12584960 | tf_op jit(solution)/shard_map/dot_general | solution.py:64
  187.3 0.0 reduce-scatter.5.cloned.1.call-update
  187.3 0.0 reduce-scatter.3.cloned.1.call-start
  187.4 8.1 %fusion.5 = f32[1536,1536]{1,0:T(8,128)} fusion(bf16[6144,2,512]{2,0,1:T(8,128)(2,1)} %all-gather.2.cloned.1.call-done, s32[]{:T(128)S(6)} %select_n.7, s32[]{:T(128)S(6)} %select_n.6), kind=kOutput, calls=%fused_computation.10 | convolution fusion | flops 2415919104 | bytes 12582920 | tf_op jit(solution)/shard_map/dot_general | solution.py:64
  195.5 0.0 reduce-scatter.3.cloned.1.call-update
  195.5 64.3 %reduce-scatter.5.cloned.1.call-done = f32[96,1536]{1,0:T(8,128)} async-done(((f32[1536,1536]{1,0:T(8,128)}), f32[96,1536]{1,0:T(8,128)}) %reduce-scatter.5.cloned.1.call-update) | async-done | bytes 589840 | tf_op jit(solution)/shard_map/reduce_scatter | solution.py:68
  259.8 1.9 broadcast_multiply_fusion
  261.7 72.8 %reduce-scatter.3.cloned.1.call-done = f32[96,1536]{1,0:T(8,128)} async-done(((f32[1536,1536]{1,0:T(8,128)}), f32[96,1536]{1,0:T(8,128)}) %reduce-scatter.3.cloned.1.call-update) | async-done | bytes 589840 | tf_op jit(solution)/shard_map/reduce_scatter | solution.py:68
  334.5 1.9 broadcast_multiply_fusion.1
  (8 shorter events, 0.1 us)
Async XLA Ops:
  7.2 4.9 %copy-start = (s32[384,2]{0,1:T(2,128)S(1)}, s32[384,2]{0,1:T(2,128)}, u32[]{:S(2)}) copy-start(s32[384,2]{0,1:T(2,128)} %param.3) | copy-start | bytes 9220
  7.2 171.9 %all-gather.2.cloned.1.call-start = ((), (), s32[]{:S(2)}) async-start(), calls=%async_computation.2 | async-start | bytes 13369344 | tf_op jit(solution)/shard_map/all_gather | solution.py:50
  9.0 3.1 collective-permute-start
  10.7 5.0 %collective-permute-start.1 = (bf16[384,2,1,128]{3,0,2,1:T(8,128)(2,1)S(1)}, bf16[384,2,1,128]{3,0,2,1:T(8,128)(2,1)S(1)}, u32[]{:S(2)}, u32[]{:S(2)}) collective-permute-start(bf16[384,2,1,128]{3,0,2,1:T(8,128)(2,1)S(1)} %get-tuple-element.9), channel_id=1, source_target_pairs={{1,0},{2,1},{3,2},{4,3},{5,4},{6,5},{7,6},{8,7},{9,8},{10,9},{11,1... | collective-permute-start | bytes 589832 | tf_op jit(solution)/shard_map/ppermute | solution.py:17
  81.4 178.4 %reduce-scatter.5.cloned.1.call-start = ((), (), s32[]{:S(2)}) async-start(), calls=%async_computation.4 | async-start | bytes 10027008 | tf_op jit(solution)/shard_map/reduce_scatter | solution.py:68
  187.3 147.2 %reduce-scatter.3.cloned.1.call-start = ((), (), s32[]{:S(2)}) async-start(), calls=%async_computation.3 | async-start | bytes 10027008 | tf_op jit(solution)/shard_map/reduce_scatter | solution.py:68
Sparse Core Ops, SparseCore 0:
  81.5 97.5 all-gather.1
  187.4 72.3 reduce-scatter.4
  262.4 72.1 reduce-scatter.2
where the time goes:
time: 343 us
  waiting for transfers between devices  239 us (70%)
  blocking collectives  62.6 us (18%)
  matrix products  16.3 us (5%)
  between operations  13.8 us (4%)
  other arithmetic  6.9 us (2%)
    reduce_scatter x2, waiting for transfers between devices, per_device(): lax.psum_scatter(partial_gram(jnp.int32(0), lax.axis_size('pix') * own_ro...  137 us
    all_gather x1, waiting for transfers between devices, per_device(): everything = lax.all_gather(normed, ('trow', 'tcol'), axis=0, tiled=True)  97.7 us
    psum x1, blocking collectives, per_device(): lax.psum(jnp.sum(shifted, axis=0), ('trow', 'tcol')) / total_frames  34.5 us
    psum x1, blocking collectives, per_device(): frame_mean = lax.psum(jnp.sum(flat, axis=(2, 3)), 'pix') / band_pixels  28 us
    dot_general x2, matrix products, partial_gram(): lax.dot_general(band_rows, band_cols, (((1,), (1,)), ((), ())), preferred...  16.3 us
  transfers between devices with their start and end apart: 5, of which 4 were waited for; matrix products, arithmetic and copies ran while one was open for 3% of the time, Pallas kernels for 0%

commit v1 on v0

v1 whole, which is shorter than its diff:
```python
import functools

import jax
import jax.numpy as jnp
from jax import lax
from jax.experimental import pallas as pl
from jax.experimental.pallas import tpu as pltpu
from jax.sharding import PartitionSpec as P

MESH = pl.DeviceIdType.MESH
SCALE = 32000.0
SUBS = 2


def remote(src, dst, send, recv, device):
    return pltpu.make_async_remote_copy(
        src_ref=src, dst_ref=dst, send_sem=send, recv_sem=recv, device_id=device, device_id_type=MESH
    )


def around(index, step, count):
    return lax.rem(index + step + count, count)


def edge_rows(cells, axis):
    count = lax.axis_size(axis)
    ends = count - 1
    head = lax.slice_in_dim(cells, 0, 1, axis=2)
    tail = lax.slice_in_dim(cells, cells.shape[2] - 1, cells.shape[2], axis=2)
    above = lax.ppermute(tail, axis, [(i, i + 1) for i in range(ends)])
    below = lax.ppermute(head, axis, [(i + 1, i) for i in range(ends)])
    return jnp.concatenate([above, cells, below], axis=2)


def blend(padded, steps, device_axis):
    upward = (jnp.maximum(steps, 0).astype(jnp.float32) / 8.0)[:, None, None, None]
    downward = (jnp.maximum(-steps, 0).astype(jnp.float32) / 8.0)[:, None, None, None]
    length = padded.shape[device_axis] - 2
    middle = lax.slice_in_dim(padded, 1, 1 + length, 1, device_axis)
    after = lax.slice_in_dim(padded, 2, 2 + length, 1, device_axis)
    before = lax.slice_in_dim(padded, 0, length, 1, device_axis)
    return (1.0 - upward - downward) * middle + upward * after + downward * before


def normalise_kernel(s_ref, n_ref, a_ref, px, py, pc, pz, xs, xr, ys, yr, cs, cr, zs, zr, *, frames, pixels):
    trow, tcol, pix = lax.axis_index("trow"), lax.axis_index("tcol"), lax.axis_index("pix")
    z, core = pix // 2, lax.rem(pix, 2)
    local = s_ref.shape[2]
    x_peers = [{"tcol": around(tcol, o, 4)} for o in (1, 2, 3)]
    y_peers = [{"trow": around(trow, o, 4)} for o in (1, 2, 3)]
    z_peers = [{"pix": around(pix, 2 * o, 16)} for o in range(1, 8)]
    partner = {"pix": pix + 1 - 2 * core}

    total = jnp.sum(s_ref[...], axis=2).reshape(8, 128)
    px[tcol] = total

    barrier = pltpu.get_barrier_semaphore()
    for device in [*x_peers, *y_peers, *z_peers, partner]:
        pl.semaphore_signal(barrier, inc=1, device_id=device, device_id_type=MESH)
    pl.semaphore_wait(barrier, 14)

    def exchange(slots, own, peers, send, recv):
        copies = [
            remote(slots.at[own], slots.at[own], send.at[i], recv.at[i], peer) for i, peer in enumerate(peers)
        ]
        for copy in copies:
            copy.start()
        for copy in copies:
            copy.wait()
        total = slots[0]
        for i in range(1, len(peers) + 1):
            total = total + slots[i]
        return total

    total = exchange(px, tcol, x_peers, xs, xr)
    py[trow] = total
    total = exchange(py, trow, y_peers, ys, yr)
    gain = frames / total

    lane = lax.broadcasted_iota(jnp.int32, (local, 128), 1)
    columns = jnp.zeros((local, 128), jnp.float32)
    for band in range(2):
        plain = jnp.zeros((local, 128), jnp.float32)
        square = jnp.zeros((local, 128), jnp.float32)
        for row in range(4):
            flat = s_ref[band, row] * gain[4 * band + row][None, :]
            plain = plain + flat
            square = square + flat * flat
        columns = jnp.where(lane == 2 * band, jnp.sum(plain, axis=1, keepdims=True), columns)
        columns = jnp.where(lane == 2 * band + 1, jnp.sum(square, axis=1, keepdims=True), columns)
    pc[core] = jnp.transpose(columns)[:8]
    pz[z] = exchange(pc, core, [partner], cs, cr)
    sums = exchange(pz, z, z_peers, zs, zr)

    for band in range(2):
        mean = sums[2 * band : 2 * band + 1] / pixels
        norm = jnp.sqrt(sums[2 * band + 1 : 2 * band + 2])
        a_ref[band : band + 1] = norm / mean * (1.0 / (SCALE * pixels) ** 0.5)
    wide = jnp.concatenate([sums, jnp.zeros((120, local), jnp.float32)], axis=0)
    tall = jnp.transpose(wide)
    for band in range(2):
        unit = (SCALE**0.5) / jnp.sqrt(tall[:, 2 * band + 1 : 2 * band + 2])
        for row in range(4):
            value = s_ref[band, row] * gain[4 * band + row][None, :] * unit
            n_ref[band, :, row * 128 : (row + 1) * 128] = value.astype(jnp.bfloat16)


def gram_kernel(
    n_ref, o_ref, rows, cols, gram, ring, handed,
    cs, cr, ls, xs, xr, x2s, x2r, ys, yr, yl, zs, zr, os_, or_,
):
    trow, tcol, pix = lax.axis_index("trow"), lax.axis_index("tcol"), lax.axis_index("pix")
    z, core = pix // 2, lax.rem(pix, 2)
    way = 1 - 2 * core
    local, half = n_ref.shape[1], n_ref.shape[2]
    sub = local // SUBS
    chunk = rows.shape[0] // 8
    east, west = {"tcol": around(tcol, 1, 4)}, {"tcol": around(tcol, -1, 4)}
    south, north = {"trow": around(trow, 1, 4)}, {"trow": around(trow, -1, 4)}
    onward, backward = {"pix": around(pix, 2 * way, 16)}, {"pix": around(pix, -2 * way, 16)}
    partner = {"pix": pix + 1 - 2 * core}

    barrier = pltpu.get_barrier_semaphore()
    for device in (east, west, south, north, onward, backward, partner):
        pl.semaphore_signal(barrier, inc=1, device_id=device, device_id_type=MESH)
    pl.semaphore_wait(barrier, 7)

    def piece(ref, block, u):
        return ref.at[pl.ds(pl.multiple_of(block * local + u * sub, sub), sub)]

    mine = pl.ds(pl.multiple_of(tcol * local, local), local)
    lanes = pl.ds(pl.multiple_of(core * half, half), half)
    keep = pltpu.make_async_copy(n_ref.at[core], rows.at[mine, lanes], ls)
    keep.start()
    give = remote(n_ref.at[1 - core], rows.at[mine, lanes], cs, cr, partner)
    give.start()
    keep.wait()
    give.wait()

    even, odd = range(0, SUBS, 2), range(1, SUBS, 2)

    def x_copy(d, u):
        place = piece(rows, tcol, u)
        return remote(place, place, xs.at[d, u], xr.at[d, u], (east, west)[d])

    def x2_copy(u):
        d = u % 2
        place = piece(rows, around(tcol, (-1, 1)[d], 4), u)
        return remote(place, place, x2s.at[u], x2r.at[u], (east, west)[d])

    offset = around(trow, -tcol, 4)
    place_on_path = (offset, around(0, -offset, 4))
    order = ((0, 3, 1, 2), (0, 1, 3, 2))

    def y_copies(m, u):
        d = u % 2
        block = around(tcol, order[d][m], 4)
        here, there = piece(rows, block, u), piece(cols, block, u)
        device = (south, north)[d]
        first = remote(here, there, ys.at[m, u], yr.at[m, u], device)
        later = remote(there, there, ys.at[m, u], yr.at[m, u], device)
        stay = pltpu.make_async_copy(here, there, yl.at[m, u])
        return first, later, stay

    def y_root(m):
        @pl.when(offset == 0)
        def _():
            for u in range(SUBS):
                first, _, stay = y_copies(m, u)
                first.start()
                stay.start()

    def y_relay(m):
        for u in range(SUBS):
            where = place_on_path[u % 2]

            @pl.when((where == 1) | (where == 2))
            def _():
                _, later, _ = y_copies(m, u)
                later.wait_recv()
                later.start()

    for u in (*even, *odd):
        x_copy(0, u).start()
    for u in (*odd, *even):
        x_copy(1, u).start()
    y_root(0)
    for u in range(SUBS):
        x_copy(u % 2, u).wait_recv()
        x2_copy(u).start()
    y_root(1)
    y_relay(0)
    for u in range(SUBS):
        x_copy(1 - u % 2, u).wait_recv()
    y_root(2)
    y_relay(1)
    for u in range(SUBS):
        x2_copy(u).wait_recv()
    y_root(3)
    y_relay(2)
    y_relay(3)

    for m in range(4):
        for u in range(SUBS):
            where = place_on_path[u % 2]

            @pl.when(where == 3)
            def _():
                y_copies(m, u)[1].wait_recv()

            @pl.when(where == 0)
            def _():
                y_copies(m, u)[2].wait()

    def block_of(o):
        return around(tcol, (0, 1, 3, 2)[o], 4)

    def part(ref, d):
        return ref.at[pl.ds(pl.multiple_of(d * chunk, chunk), chunk)]

    def multiply(o):
        right = cols.at[pl.ds(pl.multiple_of(block_of(o) * local, local), local)]

        def step(d, carry):
            product = lax.dot_general(
                part(rows, d)[...], right[...], (((1,), (1,)), ((), ())), preferred_element_type=jnp.float32
            )
            part(gram.at[o], d)[...] = jnp.round(product).astype(jnp.int32).astype(jnp.int16)
            return carry

        lax.fori_loop(0, 8, step, 0)

    def target(s):
        return lax.rem(z - way * (1 + s) + 16, 8)

    def z_first(o):
        return remote(part(gram.at[o], target(0)), ring.at[o, 0], zs.at[o, 0], zr.at[o, 0], onward)

    def z_next(o, s):
        return remote(ring.at[o, s - 1], ring.at[o, s], zs.at[o, s], zr.at[o, s], onward)

    def add(held, d, o):
        return (held[...].astype(jnp.int32) + part(gram.at[o], d)[...].astype(jnp.int32)).astype(jnp.int16)

    for o in range(4):
        multiply(o)
        z_first(o).start()

    def reduce_step(s, carry):
        for o in range(4):
            remote(ring.at[o, s - 1], ring.at[o, s - 1], zs.at[o, s - 1], zr.at[o, s - 1], onward).wait_recv()
            ring[o, s - 1] = add(ring.at[o, s - 1], target(s), o)
            z_next(o, s).start()
        return carry

    lax.fori_loop(1, 7, reduce_step, 0)

    def out_copy(o):
        place = o_ref.at[core, :, pl.ds(pl.multiple_of(block_of(o) * local, local), local)]
        return remote(handed.at[o, 1 - core], place, os_.at[o], or_.at[o], partner)

    def out_keep(o):
        place = o_ref.at[core, :, pl.ds(pl.multiple_of(block_of(o) * local, local), local)]
        return pltpu.make_async_copy(handed.at[o, core], place, yl.at[o, 0])

    for o in range(4):
        z_next(o, 6).wait_recv()
        final = add(ring.at[o, 6], z, o)
        handed[o, 0] = final[: chunk // 2]
        handed[o, 1] = final[chunk // 2 :]
        out_copy(o).start()
        out_keep(o).start()
    for o in range(4):
        out_keep(o).wait()
        out_copy(o).wait()

    for u in range(SUBS):
        x_copy(0, u).wait_send()
        x_copy(1, u).wait_send()
        x2_copy(u).wait_send()
        for m in range(4):
            @pl.when(place_on_path[u % 2] < 3)
            def _():
                y_copies(m, u)[1].wait_send()

    def sent(s, carry):
        for o in range(4):
            remote(ring.at[o, s], ring.at[o, s], zs.at[o, s], zr.at[o, s], onward).wait_send()
        return carry

    lax.fori_loop(0, 7, sent, 0)


def vmem(count):
    return [pl.BlockSpec(memory_space=pltpu.VMEM)] * count


def per_device(frames, drift):
    local, _, tile_rows, columns = frames.shape
    total_frames = local * lax.axis_size("trow") * lax.axis_size("tcol")
    band_pixels = tile_rows * columns * lax.axis_size("pix")
    padded = edge_rows(frames.astype(jnp.bfloat16), "pix").astype(frames.dtype)
    rowpass = blend(padded, drift[:, 0], 2)
    padded = jnp.pad(rowpass, ((0, 0), (0, 0), (0, 0), (1, 1)))
    shifted = blend(padded, drift[:, 1], 3).transpose(1, 2, 0, 3)

    dma = pltpu.SemaphoreType.DMA
    half = tile_rows * columns
    normed, amount = pl.pallas_call(
        functools.partial(normalise_kernel, frames=float(total_frames), pixels=float(band_pixels)),
        out_shape=(
            jax.ShapeDtypeStruct((2, local, half), jnp.bfloat16),
            jax.ShapeDtypeStruct((2, local), jnp.float32),
        ),
        in_specs=vmem(1),
        out_specs=tuple(vmem(2)),
        scratch_shapes=[
            pltpu.VMEM((4, 8, 128), jnp.float32),
            pltpu.VMEM((4, 8, 128), jnp.float32),
            pltpu.VMEM((2, 8, local), jnp.float32),
            pltpu.VMEM((8, 8, local), jnp.float32),
            dma((3,)), dma((3,)), dma((3,)), dma((3,)), dma((1,)), dma((1,)), dma((7,)), dma((7,)),
        ],
        compiler_params=pltpu.CompilerParams(collective_id=0, has_side_effects=True, vmem_limit_bytes=24 << 20),
        name="normalise",
    )(shifted)

    block = 4 * local
    summed = pl.pallas_call(
        gram_kernel,
        out_shape=jax.ShapeDtypeStruct((2, block // 16, block), jnp.int16),
        in_specs=vmem(1),
        out_specs=vmem(1)[0],
        scratch_shapes=[
            pltpu.VMEM((block, 2 * half), jnp.bfloat16),
            pltpu.VMEM((block, 2 * half), jnp.bfloat16),
            pltpu.VMEM((4, block, local), jnp.int16),
            pltpu.VMEM((4, 7, block // 8, local), jnp.int16),
            pltpu.VMEM((4, 2, block // 16, local), jnp.int16),
            dma, dma, dma,
            dma((2, SUBS)), dma((2, SUBS)), dma((SUBS,)), dma((SUBS,)),
            dma((4, SUBS)), dma((4, SUBS)), dma((4, SUBS)),
            dma((4, 7)), dma((4, 7)), dma((4,)), dma((4,)),
        ],
        compiler_params=pltpu.CompilerParams(collective_id=1, has_side_effects=True, vmem_limit_bytes=48 << 20),
        cost_estimate=pl.CostEstimate(flops=5 * 10**9, bytes_accessed=200 * 10**6, transcendentals=0),
        name="gram",
    )(normed)

    amounts = lax.all_gather(amount, ("trow", "tcol"), axis=0, tiled=False)
    pix = lax.axis_index("pix")
    by_block = amounts.reshape(4, 4, 2, local).transpose(0, 2, 1, 3).reshape(4, 2, block)
    right = lax.dynamic_index_in_dim(by_block, lax.axis_index("tcol"), 0, keepdims=False)
    left = lax.dynamic_index_in_dim(by_block, lax.axis_index("trow"), 0, keepdims=False)
    left = lax.dynamic_slice_in_dim(left, pix * (block // 16), block // 16, axis=1)
    return tuple(
        summed[band].astype(jnp.float32) * left[band][:, None] * right[band][None, :] for band in range(2)
    )


def solution(mesh):
    in_specs = (P(("trow", "tcol"), None, "pix", None), P(("trow", "tcol"), None))
    out_specs = (P(("trow", "pix"), "tcol"), P(("trow", "pix"), "tcol"))
    return jax.shard_map(
        per_device, mesh=mesh, in_specs=in_specs, out_specs=out_specs, check_vma=False
    )
```

time: 343 us -> 180 us (0.52)
  waiting for transfers between devices: 239 us -> 3.64 us
  Pallas kernels: 0 us -> 145 us
  blocking collectives: 62.6 us -> 22 us
  matrix products: 16.3 us -> 0 us
  between operations: 13.8 us -> 0.75 us
  other arithmetic: 6.9 us -> 2.87 us
    pallas_call x0 -> x2, Pallas kernels: none -> 145 us  [the longest x1 120 us: per_device(): pl.pallas_call(gram_kernel, out_shape=jax.ShapeDtypeStruct((2, block // 1...]
    reduce_scatter x2 -> x0, waiting for transfers between devices: 137 us -> none  [per_device(): lax.psum_scatter(partial_gram(jnp.int32(0), lax.axis_size('pix') * own_ro...]
    all_gather x1 -> x0, waiting for transfers between devices: 97.7 us -> none  [per_device(): everything = lax.all_gather(normed, ('trow', 'tcol'), axis=0, tiled=True)]
    psum x2 -> x0, blocking collectives: 62.6 us -> none  [the longest x1 34.5 us: per_device(): lax.psum(jnp.sum(shifted, axis=0), ('trow', 'tcol')) / total_frames]
    all_gather x0 -> x1, blocking collectives: none -> 22 us  [per_device(): amounts = lax.all_gather(amount, ('trow', 'tcol'), axis=0, tiled=False)]
    dot_general x2 -> x0, matrix products: 16.3 us -> none  [partial_gram(): lax.dot_general(band_rows, band_cols, (((1,), (1,)), ((), ())), preferred...]
    div x4 -> x0, other arithmetic: 3.86 us -> none  [the longest x2 3.85 us: per_device(): results.append(summed / band_pixels)]
  transfers between devices with their start and end apart: 5 -> 2, of which waited for: 4 -> 1; matrix products, arithmetic and copies ran while one was open for 3% -> 0% of each run, Pallas kernels for 0% -> 0%
where the time goes in v1:
time: 180 us
  Pallas kernels  145 us (81%)
  blocking collectives  22 us (12%)
  waiting for transfers between devices  3.64 us (2%)
  starting transfers between devices  3.04 us (2%)
  other arithmetic  2.87 us (2%)
  local copies, waits for them, and re-layouts  1.87 us (1%)
    pallas_call x1, Pallas kernels, per_device(): pl.pallas_call(gram_kernel, out_shape=jax.ShapeDtypeStruct((2, block // 1...  120 us
    pallas_call x1, Pallas kernels, per_device(): pl.pallas_call(functools.partial(normalise_kernel, frames=float(total_fra...  25.2 us
    all_gather x1, blocking collectives, per_device(): amounts = lax.all_gather(amount, ('trow', 'tcol'), axis=0, tiled=False)  22 us
    ppermute x1, waiting for transfers between devices, edge_rows(): below = lax.ppermute(head, axis, [(i + 1, i) for i in range(ends)])  3.64 us
  transfers between devices with their start and end apart: 2, of which 1 were waited for; matrix products, arithmetic and copies ran while one was open for 0% of the time, Pallas kernels for 0%

profile of v1, /device:TPU:8, one launch (start us, length us, event | category | flops | bytes accessed | tf_op | source)
XLA Modules:
  0.0 179.6 jit_solution(12598303474718595044)
XLA Ops:
  0.6 0.0 copy-start
  0.6 1.7 copy.7
  2.4 1.8 collective-permute-start
  4.2 1.3 collective-permute-start.1
  5.5 0.0 copy-done
  5.5 0.0 collective-permute-done
  5.5 3.6 %collective-permute-done.1 = bf16[384,2,1,128]{3,0,2,1:T(8,128)(2,1)S(1)} collective-permute-done((bf16[384,2,1,128]{3,0,2,1:T(8,128)(2,1)S(1)}, bf16[384,2,1,128]{3,0,2,1:T(8,128)(2,1)S(1)}, u32[]{:S(2)}, u32[]{:S(2)}) %collective-permute-start.1) | collective-permute-done | bytes 196640 | tf_op jit(solution)/shard_map/ppermute | solution.py:31
  9.2 0.2 maximum_convert_fusion
  9.4 0.4 fusion.5
  9.7 1.0 fusion.3.s_ref
  10.8 25.2 %normalise.1 = (bf16[2,384,512]{2,1,0:T(8,128)(2,1)S(1)}, f32[2,384]{1,0:T(2,128)S(1)}) custom-call(f32[2,4,384,128]{3,2,1,0:T(8,128)S(1)} %fusion.3.s_ref), custom_call_target="tpu_custom_call" | custom-call | tf_op jit(solution)/shard_map/normalise/pallas_call | solution.py:309
  36.0 22.0 %all-gather.1 = f32[16,2,384]{2,1,0:T(2,128)S(1)} all-gather(f32[1,2,384]{2,1,0:T(2,128)S(1)} %bitcast.18), channel_id=2, replica_groups=mesh['trow'=4,'tcol'=4,'pix'=16] {'trow','tcol'}, dimensions={0}, use_global_device_ids=true | all-gather | bytes 52224 | tf_op jit(solution)/shard_map/all_gather | solution.py:350
  57.9 0.1 constant_dynamic-slice_fusion
  58.0 120.3 %gram.1 = s16[2,96,1536]{2,1,0:T(8,128)(2,1)S(1)} custom-call(bf16[2,384,512]{2,1,0:T(8,128)(2,1)S(1)} %get-tuple-element.4.n_ref), custom_call_target="tpu_custom_call" | custom-call | flops 5000000000 | bytes 200000000 | tf_op jit(solution)/shard_map/gram/pallas_call | solution.py:329
  178.3 1.2 fusion.7
  (5 shorter events, 0.1 us)
Async XLA Ops:
  0.6 4.8 %copy-start = (s32[384,2]{0,1:T(2,128)S(1)}, s32[384,2]{0,1:T(2,128)}, u32[]{:S(2)}) copy-start(s32[384,2]{0,1:T(2,128)} %param.3) | copy-start | bytes 9220
  2.4 3.1 %collective-permute-start = (bf16[384,2,1,128]{3,0,2,1:T(8,128)(2,1)S(1)}, bf16[384,2,1,128]{3,0,2,1:T(8,128)(2,1)S(1)}, u32[]{:S(2)}, u32[]{:S(2)}) collective-permute-start(bf16[384,2,1,128]{3,0,2,1:T(8,128)(2,1)S(1)} %get-tuple-element.12), channel_id=1, source_target_pairs={{0,1},{1,2},{2,3},{3,4},{4,5},{5,6},{6,7},{7,8},{8,9},{9,10},{10,1... | collective-permute-start | bytes 589832 | tf_op jit(solution)/shard_map/ppermute | solution.py:30
  4.2 5.0 %collective-permute-start.1 = (bf16[384,2,1,128]{3,0,2,1:T(8,128)(2,1)S(1)}, bf16[384,2,1,128]{3,0,2,1:T(8,128)(2,1)S(1)}, u32[]{:S(2)}, u32[]{:S(2)}) collective-permute-start(bf16[384,2,1,128]{3,0,2,1:T(8,128)(2,1)S(1)} %get-tuple-element.13), channel_id=1, source_target_pairs={{1,0},{2,1},{3,2},{4,3},{5,4},{6,5},{7,6},{8,7},{9,8},{10,9},{11,1... | collective-permute-start | bytes 589832 | tf_op jit(solution)/shard_map/ppermute | solution.py:31

commit v2 on v0

v2 whole, which is shorter than its diff:
```python
import functools

import jax
import jax.numpy as jnp
from jax import lax
from jax.experimental import pallas as pl
from jax.experimental.pallas import tpu as pltpu
from jax.sharding import PartitionSpec as P

MESH = pl.DeviceIdType.MESH
SCALE = 32000.0
OWN, WEST, EAST, FAR = range(4)
PATHS = (
    ((OWN, 0), (OWN, 1), (WEST, 0), (EAST, 0), (WEST, 1), (EAST, 1), (FAR, 0), (FAR, 1)),
    ((OWN, 0), (OWN, 1), (EAST, 0), (WEST, 0), (EAST, 1), (WEST, 1), (FAR, 0), (FAR, 1)),
)
STREAMS = [(0, OWN), (1, OWN), (0, WEST), (0, EAST), (1, WEST), (1, EAST), (0, FAR), (1, FAR)]


def remote(src, dst, send, recv, device):
    return pltpu.make_async_remote_copy(
        src_ref=src, dst_ref=dst, send_sem=send, recv_sem=recv, device_id=device, device_id_type=MESH
    )


def around(index, step, count):
    return lax.rem(index + step + count, count)


def twotime_kernel(
    x_ref, w_ref, o_ref,
    halo, s, give, rows, cols, gram, ring, handed, px, py, pc, pz, rsum, csum, rq, cq,
    hs, hr, pxs, pxr, pys, pyr, gs, gr, xs, xr, x2s, x2r, ys, yr, yl,
    pcs, pcr, pzs, pzr, rss, rsr, css, csr, zs, zr, os_, or_,
    *, frames, pixels,
):
    trow, tcol, pix = lax.axis_index("trow"), lax.axis_index("tcol"), lax.axis_index("pix")
    z, core = pix // 2, lax.rem(pix, 2)
    way = 1 - 2 * core
    local = x_ref.shape[2]
    sub = local // 4
    half = 4 * 128
    x_peers = [{"tcol": around(tcol, i, 4)} for i in (1, 2, 3)]
    y_peers = [{"trow": around(trow, i, 4)} for i in (1, 2, 3)]
    z_peers = [{"pix": around(pix, 2 * i, 16)} for i in range(1, 8)]
    east, west = x_peers[0], x_peers[2]
    south, north = y_peers[0], y_peers[2]
    onward = {"pix": around(pix, 2 * way, 16)}
    partner = {"pix": pix + way}
    other = {"pix": around(pix, -way, 16)}
    above, below = {"pix": around(pix, -1, 16)}, {"pix": around(pix, 1, 16)}

    barrier = pltpu.get_barrier_semaphore()
    for device in [*x_peers, *y_peers, *z_peers, partner, other]:
        pl.semaphore_signal(barrier, inc=1, device_id=device, device_id_type=MESH)
    pl.semaphore_wait(barrier, 15)

    edges = [
        remote(x_ref.at[:, 3], halo.at[0], hs.at[0], hr.at[0], below),
        remote(x_ref.at[:, 0], halo.at[1], hs.at[1], hr.at[1], above),
    ]
    for copy in edges:
        copy.start()
    for copy in edges:
        copy.wait()
    lane = lax.broadcasted_iota(jnp.int32, (sub, 128), 1)
    has_above = (pix > 0).astype(jnp.float32)
    has_below = (pix < 15).astype(jnp.float32)
    sums = [[jnp.zeros((8, 128), jnp.float32) for _ in range(4)] for _ in range(2)]
    for band in range(2):
        for t in range(4):
            at = pl.ds(t * sub, sub)
            stay_r, up_r, down_r, stay_c, up_c, down_c = (w_ref[at, i : i + 1] for i in range(6))
            up_c = jnp.where(lane < 127, up_c, 0.0)
            down_c = jnp.where(lane > 0, down_c, 0.0)
            line = [halo[0, band, at, :].astype(jnp.float32) * has_above]
            line += [x_ref[band, r, at, :].astype(jnp.float32) for r in range(4)]
            line += [halo[1, band, at, :].astype(jnp.float32) * has_below]
            for r in range(4):
                mid = stay_r * line[r + 1] + up_r * line[r + 2] + down_r * line[r]
                moved = stay_c * mid + up_c * pltpu.roll(mid, 127, 1) + down_c * pltpu.roll(mid, 1, 1)
                s[band, r, at, :] = moved
                sums[band][r] += jnp.sum(moved.reshape(sub // 8, 8, 128), axis=0)
    for band in range(2):
        for r in range(4):
            px[tcol, 4 * band + r] = jnp.sum(sums[band][r], axis=0)

    def exchange(slots, own, peers, send, recv):
        return [remote(slots.at[own], slots.at[own], send.at[i], recv.at[i], peer) for i, peer in enumerate(peers)]

    def add_up(slots, count):
        total = slots[0]
        for i in range(1, count):
            total = total + slots[i]
        return total

    def meet(slots, own, peers, send, recv):
        copies = exchange(slots, own, peers, send, recv)
        for copy in copies:
            copy.start()
        for copy in copies:
            copy.wait()
        return add_up(slots, len(peers) + 1)

    py[trow] = meet(px, tcol, x_peers, pxs, pxr)
    px[tcol] = frames / meet(py, trow, y_peers, pys, pyr)

    def gain(band, r):
        return px[tcol, pl.ds(4 * band + r, 1), :]

    def row_piece(block, e, h):
        return pl.ds(pl.multiple_of((2 * block + e) * sub, sub), sub)

    def col_piece(block, e, h):
        return pl.ds(pl.multiple_of(block * local + (2 * e + h) * sub, sub), sub)

    pieces = [(e, h) for h in range(2) for e in range(2)]
    lanes = pl.ds(pl.multiple_of(core * half, half), half)

    def give_copy(e, h):
        return remote(give.at[h, e], rows.at[h, row_piece(tcol, e, h), lanes], gs.at[h, e], gr.at[h, e], partner)

    for e, h in pieces:
        at = pl.ds((2 * e + h) * sub, sub)
        for r in range(4):
            flat = s[1 - core, r, at, :] * gain(1 - core, r)
            give[h, e, :, r * 128 : (r + 1) * 128] = flat.astype(jnp.bfloat16)
        give_copy(e, h).start()
    for e, h in pieces:
        at = pl.ds((2 * e + h) * sub, sub)
        for r in range(4):
            flat = s[core, r, at, :] * gain(core, r)
            place = pl.ds(pl.multiple_of(core * half + r * 128, 128), 128)
            rows[h, row_piece(tcol, e, h), place] = flat.astype(jnp.bfloat16)

    def x_copy(d, e, h):
        place = rows.at[h, row_piece(tcol, e, h)]
        return remote(place, place, xs.at[d, e, h], xr.at[d, e, h], (east, west)[d])

    def x2_copy(e, h):
        place = rows.at[h, row_piece(around(tcol, (-1, 1)[e], 4), e, h)]
        return remote(place, place, x2s.at[e, h], x2r.at[e, h], (east, west)[e])

    offset = around(trow, -tcol, 4)
    position = (offset, around(0, -offset, 4))

    def block_of(o):
        return around(tcol, (0, -1, 1, 2)[o], 4)

    def y_copies(d, i):
        o, h = PATHS[d][i]
        here, there = rows.at[h, row_piece(block_of(o), d, h)], cols.at[col_piece(block_of(o), d, h)]
        device = (south, north)[d]
        return here, there, device, ys.at[d, i], yr.at[d, i]

    def y_next(d, i):
        _, there, device, send, recv = y_copies(d, i)
        return remote(there, there, send, recv, device)

    def y_stay(d, i):
        here, there, _, _, _ = y_copies(d, i)
        return pltpu.make_async_copy(here, there, yl.at[d, i])

    def y_tick(tick):
        if tick < 8:
            @pl.when(offset == 0)
            def _():
                for d in range(2):
                    here, there, device, send, recv = y_copies(d, tick)
                    remote(here, there, send, recv, device).start()
                    y_stay(d, tick).start()

        for far in (1, 2):
            if 0 <= tick - far < 8:
                for d in range(2):
                    @pl.when(position[d] == far)
                    def _():
                        y_next(d, tick - far).wait_recv()
                        y_next(d, tick - far).start()

    def y_arrived(first, last):
        for i in range(first, last):
            for d in range(2):
                @pl.when(position[d] == 3)
                def _():
                    y_next(d, i).wait_recv()

                @pl.when(position[d] == 0)
                def _():
                    y_stay(d, i).wait()

    def x_start(h):
        x_copy(0, 0, h).start()
        x_copy(1, 1, h).start()
        x_copy(0, 1, h).start()
        x_copy(1, 0, h).start()

    def x_pass(h):
        for e in range(2):
            x_copy(e, e, h).wait_recv()
            x2_copy(e, h).start()

    def chunk(i, d):
        return gram.at[i, pl.ds(pl.multiple_of(d * sub, sub), sub)]

    def target(step):
        return lax.rem(z - way * (1 + step) + 16, 8)

    def multiply(i):
        h, o = STREAMS[i]
        right = cols.at[pl.ds(pl.multiple_of(block_of(o) * local, local), local)]
        scale = cq[o, 0:1]

        def step(t, carry):
            at = pl.ds(pl.multiple_of(t * 2 * sub, 2 * sub), 2 * sub)
            product = lax.dot_general(
                rows[h, at, :], right[...], (((1,), (1,)), ((), ())), preferred_element_type=jnp.float32
            )
            product = product * rq[h, at, 0:1] * scale
            gram[i, at, :] = jnp.round(product).astype(jnp.int32).astype(jnp.int16)
            return carry

        lax.fori_loop(0, 4, step, 0)
        remote(chunk(i, target(0)), ring.at[i, 0], zs.at[i, 0], zr.at[i, 0], onward).start()

    def z_copy(i, step):
        return remote(ring.at[i, step - 1], ring.at[i, step], zs.at[i, step], zr.at[i, step], onward)

    def arrived(i, step):
        remote(ring.at[i, step - 1], ring.at[i, step - 1], zs.at[i, step - 1], zr.at[i, step - 1], onward).wait_recv()

    def out_place(o, band):
        return o_ref.at[band, :, pl.ds(pl.multiple_of(block_of(o) * local, local), local)]

    def advance(i, step):
        h, o = STREAMS[i]
        arrived(i, step)
        if step < 7:
            ring[i, step - 1] = (
                ring[i, step - 1].astype(jnp.int32) + chunk(i, target(step))[...].astype(jnp.int32)
            ).astype(jnp.int16)
            z_copy(i, step).start()
            return
        final = (ring[i, 6].astype(jnp.int32) + chunk(i, z)[...].astype(jnp.int32)).astype(jnp.float32)
        at = pl.ds(pl.multiple_of(z * sub, sub), sub)
        handed[i] = final * rq[h, at, 1:2] * cq[o, 1:2]

        @pl.when(core != h)
        def _():
            remote(handed.at[i], out_place(o, core), os_.at[i], or_.at[o], partner).start()

        @pl.when(core == h)
        def _():
            pltpu.make_async_copy(handed.at[i], out_place(o, core), os_.at[i]).start()

    def frame_sums():
        wide = lax.broadcasted_iota(jnp.int32, (sub, 128), 1)
        for t in range(4):
            at = pl.ds(t * sub, sub)
            columns = jnp.zeros((sub, 128), jnp.float32)
            for band in range(2):
                plain = jnp.zeros((sub, 128), jnp.float32)
                square = jnp.zeros((sub, 128), jnp.float32)
                for r in range(4):
                    flat = s[band, r, at, :] * gain(band, r)
                    plain = plain + flat
                    square = square + flat * flat
                columns = jnp.where(wide == 2 * band, jnp.sum(plain, axis=1, keepdims=True), columns)
                columns = jnp.where(wide == 2 * band + 1, jnp.sum(square, axis=1, keepdims=True), columns)
            s[0, 0, at, :] = columns
        pc[core] = jnp.transpose(s[0, 0])[:8]

    def scales(total):
        plain = jnp.where(core == 0, total[0:1], total[2:3])
        norm = jnp.sqrt(jnp.where(core == 0, total[1:2], total[3:4]))
        quant = (SCALE**0.5) / norm
        amount = norm * (pixels / (SCALE * pixels) ** 0.5) / plain
        return jnp.concatenate([quant, amount, jnp.zeros((6, local), jnp.float32)], axis=0)

    for e, h in pieces[:2]:
        give_copy(e, h).wait_recv()
    x_start(0)
    for e, h in pieces[2:]:
        give_copy(e, h).wait_recv()
    y_tick(0)
    frame_sums()
    partner_sums = exchange(pc, core, [partner], pcs, pcr)
    partner_sums[0].start()
    x_pass(0)
    x_start(1)
    y_tick(1)
    partner_sums[0].wait_recv()
    pz[z] = add_up(pc, 2)
    z_sums = exchange(pz, z, z_peers, pzs, pzr)
    for copy in z_sums:
        copy.start()
    for e in range(2):
        x_copy(1 - e, e, 0).wait_recv()
    y_tick(2)
    for copy in z_sums:
        copy.wait_recv()
    rsum[tcol] = scales(add_up(pz, 8))
    x_sums = exchange(rsum, tcol, x_peers, rss, rsr)
    for copy in x_sums:
        copy.start()
    for e in range(2):
        x2_copy(e, 0).wait_recv()
    y_tick(3)
    for copy in x_sums:
        copy.wait_recv()
    y_sums = [remote(rsum, csum, css.at[i], csr.at[i], peer) for i, peer in enumerate(y_peers)]

    @pl.when(offset == 0)
    def _():
        for copy in y_sums:
            copy.start()

    for block in range(4):
        tall = jnp.transpose(jnp.concatenate([rsum[block], jnp.zeros((120, local), jnp.float32)], axis=0))
        for e, h in pieces:
            rq[h, (2 * block + e) * sub : (2 * block + e + 1) * sub, :] = tall[(2 * e + h) * sub : (2 * e + h + 1) * sub]
    x_pass(1)
    y_tick(4)
    for i in range(3):
        @pl.when(offset == i + 1)
        def _():
            y_sums[i].wait_recv()

    for o in range(4):
        cq[o] = jnp.where(offset == 0, rsum[block_of(o)], csum[block_of(o)])
    y_arrived(0, 2)
    multiply(0)
    for e in range(2):
        x_copy(1 - e, e, 1).wait_recv()
    y_tick(5)
    advance(0, 1)
    for e in range(2):
        x2_copy(e, 1).wait_recv()
    y_tick(6)
    multiply(1)
    advance(0, 2)
    y_tick(7)
    advance(1, 1)
    advance(0, 3)
    advance(1, 2)
    y_tick(8)
    advance(0, 4)
    advance(1, 3)
    y_arrived(2, 6)
    for i in (2, 3):
        multiply(i)
    advance(0, 5)
    advance(1, 4)
    y_tick(9)
    for i in (4, 5):
        multiply(i)
    done = [5, 4, 0, 0, 0, 0, 0, 0]
    live = [0, 1, 2, 3, 4, 5]
    rounds = 0
    while min(done) < 7:
        for i in live:
            if done[i] < 7:
                done[i] += 1
                advance(i, done[i])
        rounds += 1
        if rounds == 1:
            y_arrived(6, 8)
            for i in (6, 7):
                multiply(i)
            live = list(range(8))

    for i, (h, o) in enumerate(STREAMS):
        @pl.when(core != h)
        def _():
            remote(handed.at[i], out_place(o, core), os_.at[i], or_.at[o], partner).wait_send()

        @pl.when(core == h)
        def _():
            pltpu.make_async_copy(handed.at[i], out_place(o, core), os_.at[i]).wait()
            remote(handed.at[i], out_place(o, 1 - core), os_.at[i], or_.at[o], partner).wait_recv()

    for e, h in pieces:
        give_copy(e, h).wait_send()
        x_copy(0, e, h).wait_send()
        x_copy(1, e, h).wait_send()
        x2_copy(e, h).wait_send()
    for d in range(2):
        @pl.when(position[d] < 3)
        def _():
            for i in range(8):
                y_next(d, i).wait_send()

    for copy in [*partner_sums, *z_sums, *x_sums]:
        copy.wait_send()

    @pl.when(offset == 0)
    def _():
        for copy in y_sums:
            copy.wait_send()

    def sent(step, carry):
        for i in range(8):
            remote(ring.at[i, step], ring.at[i, step], zs.at[i, step], zr.at[i, step], onward).wait_send()
        return carry

    lax.fori_loop(0, 7, sent, 0)


def per_device(frames, drift):
    local, _, tile_rows, columns = frames.shape
    total_frames = local * lax.axis_size("trow") * lax.axis_size("tcol")
    band_pixels = tile_rows * columns * lax.axis_size("pix")
    plain = frames.astype(jnp.bfloat16).transpose(1, 2, 0, 3)
    up = jnp.maximum(drift, 0).astype(jnp.float32) / 8.0
    down = jnp.maximum(-drift, 0).astype(jnp.float32) / 8.0
    stay = 1.0 - up - down
    weights = jnp.stack([stay[:, 0], up[:, 0], down[:, 0], stay[:, 1], up[:, 1], down[:, 1]], axis=1)

    dma = pltpu.SemaphoreType.DMA
    vmem = pl.BlockSpec(memory_space=pltpu.VMEM)
    block, half, sub = 4 * local, tile_rows * columns, local // 4
    f32, bf16, i16 = jnp.float32, jnp.bfloat16, jnp.int16
    out = pl.pallas_call(
        functools.partial(twotime_kernel, frames=float(total_frames), pixels=float(band_pixels)),
        out_shape=jax.ShapeDtypeStruct((2, block // 16, block), jnp.float32),
        in_specs=[vmem, vmem],
        out_specs=vmem,
        scratch_shapes=[
            pltpu.VMEM((2, 2, local, columns), bf16),
            pltpu.VMEM((2, tile_rows, local, columns), f32),
            pltpu.VMEM((2, 2, sub, half), bf16),
            pltpu.VMEM((2, block // 2, 2 * half), bf16),
            pltpu.VMEM((block, 2 * half), bf16),
            pltpu.VMEM((8, block // 2, local), i16),
            pltpu.VMEM((8, 7, sub, local), i16),
            pltpu.VMEM((8, sub, local), f32),
            pltpu.VMEM((4, 8, columns), f32),
            pltpu.VMEM((4, 8, columns), f32),
            pltpu.VMEM((2, 8, local), f32),
            pltpu.VMEM((8, 8, local), f32),
            pltpu.VMEM((4, 8, local), f32),
            pltpu.VMEM((4, 8, local), f32),
            pltpu.VMEM((2, block // 2, 128), f32),
            pltpu.VMEM((4, 8, local), f32),
            dma((2,)), dma((2,)), dma((3,)), dma((3,)), dma((3,)), dma((3,)), dma((2, 2)), dma((2, 2)),
            dma((2, 2, 2)), dma((2, 2, 2)), dma((2, 2)), dma((2, 2)), dma((2, 8)), dma((2, 8)), dma((2, 8)),
            dma((1,)), dma((1,)), dma((7,)), dma((7,)), dma((3,)), dma((3,)), dma((3,)), dma((3,)),
            dma((8, 7)), dma((8, 7)), dma((8,)), dma((4,)),
        ],
        compiler_params=pltpu.CompilerParams(collective_id=0, has_side_effects=True, vmem_limit_bytes=48 << 20),
        name="twotime",
    )(plain, weights)
    return out[0], out[1]


def solution(mesh):
    in_specs = (P(("trow", "tcol"), None, "pix", None), P(("trow", "tcol"), None))
    out_specs = (P(("trow", "pix"), "tcol"), P(("trow", "pix"), "tcol"))
    return jax.shard_map(
        per_device, mesh=mesh, in_specs=in_specs, out_specs=out_specs, check_vma=False
    )
```

time: 343 us -> 127 us (0.37)
  waiting for transfers between devices: 239 us -> 0 us
  Pallas kernels: 0 us -> 121 us
  blocking collectives: 62.6 us -> 0 us
  matrix products: 16.3 us -> 0 us
  between operations: 13.8 us -> 0.66 us
  other arithmetic: 6.9 us -> 0.69 us
    reduce_scatter x2 -> x0, waiting for transfers between devices: 137 us -> none  [per_device(): lax.psum_scatter(partial_gram(jnp.int32(0), lax.axis_size('pix') * own_ro...]
    pallas_call x0 -> x1, Pallas kernels: none -> 121 us  [per_device(): pl.pallas_call(functools.partial(twotime_kernel, frames=float(total_frame...]
    all_gather x1 -> x0, waiting for transfers between devices: 97.7 us -> none  [per_device(): everything = lax.all_gather(normed, ('trow', 'tcol'), axis=0, tiled=True)]
    psum x2 -> x0, blocking collectives: 62.6 us -> none  [the longest x1 34.5 us: per_device(): lax.psum(jnp.sum(shifted, axis=0), ('trow', 'tcol')) / total_frames]
    dot_general x2 -> x0, matrix products: 16.3 us -> none  [partial_gram(): lax.dot_general(band_rows, band_cols, (((1,), (1,)), ((), ())), preferred...]
    ppermute x2 -> x0, waiting for transfers between devices: 3.66 us -> none  [the longest x1 3.66 us: extended(): lax.ppermute(head, axis, [((i + 1) % count, i) for i in range(ends)])]
  transfers between devices with their start and end apart: 5 -> 0, of which waited for: 4 -> 0; matrix products, arithmetic and copies ran while one was open for 3% -> 0% of each run, Pallas kernels for 0% -> 0%
where the time goes in v2:
time: 127 us; the launch traced here: 125 us
  Pallas kernels  121 us (95%)
  local copies, waits for them, and re-layouts  2.99 us (2%)
    pallas_call x1, Pallas kernels, per_device(): pl.pallas_call(functools.partial(twotime_kernel, frames=float(total_frame...  121 us

profile of v2, /device:TPU:8, one launch (start us, length us, event | category | flops | bytes accessed | tf_op | source)
XLA Modules:
  0.0 125.3 jit_solution(6284544236730514771)
XLA Ops:
  0.6 0.7 convert_multiply_fusion
  1.4 0.1 copy.8.w_ref
  1.5 1.7 %copy.12 = bf16[384,2,4,128]{3,0,2,1:T(8,128)(2,1)S(1)} copy(f32[384,2,4,128]{3,2,1,0:T(4,128)} %param.2) | data formatting | bytes 2359296 | tf_op args[0]
  3.2 121.0 %twotime.1 = f32[2,96,1536]{2,1,0:T(8,128)S(1)} custom-call(bf16[2,4,384,128]{3,2,1,0:T(8,128)(2,1)S(1)} %bitcast.7, f32[384,6]{1,0:T(8,128)S(1)} %copy.8.w_ref), custom_call_target="tpu_custom_call" | custom-call | tf_op jit(solution)/shard_map/twotime/pallas_call | solution.py:423
  124.2 1.1 slice_bitcast_fusion
  (3 shorter events, 0.0 us)

commit v3 on v2

v3 whole, which is shorter than its diff:
```python
import functools

import jax
import jax.numpy as jnp
from jax import lax
from jax.experimental import pallas as pl
from jax.experimental.pallas import tpu as pltpu
from jax.sharding import PartitionSpec as P

MESH = pl.DeviceIdType.MESH
SCALE = 32000.0
OWN, WEST, EAST, FAR = range(4)
PATHS = tuple(
    tuple((o, band) for band in range(2) for o in blocks)
    for blocks in ((OWN, WEST, EAST, FAR), (OWN, EAST, WEST, FAR))
)
STREAMS = [(band, o) for band in range(2) for o in (OWN, WEST, EAST, FAR)]


def remote(src, dst, send, recv, device):
    return pltpu.make_async_remote_copy(
        src_ref=src, dst_ref=dst, send_sem=send, recv_sem=recv, device_id=device, device_id_type=MESH
    )


def around(index, step, count):
    return lax.rem(index + step + count, count)


def plan(tick, take_sums, y_arrived, multiply, start, advance):
    beat, hop, wire = 5.0, 2.5, 1.5
    todo = [(beat * t, 0, lambda t=t: tick(t)) for t in range(10)]
    ready = [beat * t for t in (4.4, 5.6, 5.7, 6.8, 7.6, 9.5, 9.6, 10.7)]
    clock, free, events = 0.0, 0.0, []
    for i, when in enumerate(ready):
        heads = [lambda: None]
        if i == 0:
            heads = [take_sums, lambda: y_arrived(0, 1)]
        elif i in (1, 3, 5, 7):
            heads = [lambda i=i: y_arrived(*((1, 3), (3, 4), (5, 7), (7, 8))[i // 2])]
        elif i == 4:
            heads = [lambda: y_arrived(4, 5)]
        for head in heads:
            todo.append((when, 1, head))
        todo.append((when, 2, lambda i=i: multiply(i)))
        events.append((when + 2.5, i, 0))
    while events:
        events.sort()
        when, i, step = events.pop(0)
        clock = max(clock + 0.3, when)
        todo.append((clock, 3, (lambda i=i: start(i)) if step == 0 else (lambda i=i, step=step: advance(i, step))))
        if step < 4:
            free = max(free, clock) + wire
            events.append((free + hop, i, step + 1))
    return [run for _, _, run in sorted(todo, key=lambda item: item[:2])]


def twotime_kernel(
    x_ref, w_ref, o_ref,
    halo, s, rows, cols, gram, mate, ring, px, py, pc, pz, rsum, csum, rq, cq,
    hs, hr, pxs, pxr, pys, pyr, ms, mr, xs, xr, x2s, x2r, ys, yr, yl,
    pcs, pcr, pzs, pzr, rss, rsr, css, csr, zs, zr,
    *, frames, pixels,
):
    trow, tcol, pix = lax.axis_index("trow"), lax.axis_index("tcol"), lax.axis_index("pix")
    z, core = pix // 2, lax.rem(pix, 2)
    way = 1 - 2 * core
    local = x_ref.shape[2]
    sub = local // 4
    half = 4 * 128
    x_peers = [{"tcol": around(tcol, i, 4)} for i in (1, 2, 3)]
    y_peers = [{"trow": around(trow, i, 4)} for i in (1, 2, 3)]
    z_peers = [{"pix": around(pix, 2 * i, 16)} for i in range(1, 8)]
    east, west = x_peers[0], x_peers[2]
    south, north = y_peers[0], y_peers[2]
    onward, backward = {"pix": around(pix, 2 * way, 16)}, {"pix": around(pix, -2 * way, 16)}
    partner = {"pix": pix + way}
    other = {"pix": around(pix, -way, 16)}
    above, below = {"pix": around(pix, -1, 16)}, {"pix": around(pix, 1, 16)}

    barrier = pltpu.get_barrier_semaphore()
    for device in [*x_peers, *y_peers, *z_peers, partner, other]:
        pl.semaphore_signal(barrier, inc=1, device_id=device, device_id_type=MESH)
    pl.semaphore_wait(barrier, 15)

    edges = [
        remote(x_ref.at[:, 3], halo.at[0], hs.at[0], hr.at[0], below),
        remote(x_ref.at[:, 0], halo.at[1], hs.at[1], hr.at[1], above),
    ]
    for copy in edges:
        copy.start()
    lane = lax.broadcasted_iota(jnp.int32, (sub, 128), 1)
    has_above = (pix > 0).astype(jnp.float32)
    has_below = (pix < 15).astype(jnp.float32)
    sums = [[jnp.zeros((8, 128), jnp.float32) for _ in range(4)] for _ in range(2)]
    for inner in (True, False):
        if not inner:
            for copy in edges:
                copy.wait()
        for t in range(4):
            at = pl.ds(t * sub, sub)
            stay_r, up_r, down_r, stay_c, up_c, down_c = (w_ref[at, i : i + 1] for i in range(6))
            up_c = jnp.where(lane < 127, up_c, 0.0)
            down_c = jnp.where(lane > 0, down_c, 0.0)
            for band in range(2):
                line = {r + 1: x_ref[band, r, at, :].astype(jnp.float32) for r in range(4)}
                if not inner:
                    line[0] = halo[0, band, at, :].astype(jnp.float32) * has_above
                    line[5] = halo[1, band, at, :].astype(jnp.float32) * has_below
                for r in (1, 2) if inner else (0, 3):
                    mid = stay_r * line[r + 1] + up_r * line[r + 2] + down_r * line[r]
                    moved = stay_c * mid + up_c * pltpu.roll(mid, 127, 1) + down_c * pltpu.roll(mid, 1, 1)
                    s[band, r, at, :] = moved
                    sums[band][r] += jnp.sum(moved.reshape(sub // 8, 8, 128), axis=0)
    for band in range(2):
        for r in range(4):
            px[tcol, 4 * band + r] = jnp.sum(sums[band][r], axis=0)

    def exchange(slots, own, peers, send, recv):
        return [remote(slots.at[own], slots.at[own], send.at[i], recv.at[i], peer) for i, peer in enumerate(peers)]

    def add_up(slots, count):
        total = slots[0]
        for i in range(1, count):
            total = total + slots[i]
        return total

    def meet(slots, own, peers, send, recv):
        copies = exchange(slots, own, peers, send, recv)
        for copy in copies:
            copy.start()
        for copy in copies:
            copy.wait()
        return add_up(slots, len(peers) + 1)

    py[trow] = meet(px, tcol, x_peers, pxs, pxr)
    px[tcol] = frames / meet(py, trow, y_peers, pys, pyr)

    def gain(band, r):
        return px[tcol, pl.ds(4 * band + r, 1), :]

    def part_of(block, e):
        return 2 * block + e

    def flatten(band):
        for e in range(2):
            for h in range(2):
                at = pl.ds((2 * e + h) * sub, sub)
                for r in range(4):
                    flat = s[band, r, at, :] * gain(band, r)
                    rows[band, part_of(tcol, e), h, :, r * 128 : (r + 1) * 128] = flat.astype(jnp.bfloat16)

    def x_copy(d, e, band):
        place = rows.at[band, part_of(tcol, e)]
        return remote(place, place, xs.at[d, e, band], xr.at[d, e, band], (east, west)[d])

    def x2_copy(e, band):
        place = rows.at[band, part_of(around(tcol, (-1, 1)[e], 4), e)]
        return remote(place, place, x2s.at[e, band], x2r.at[e, band], (east, west)[e])

    offset = around(trow, -tcol, 4)
    position = (offset, around(0, -offset, 4))

    def block_of(o):
        return around(tcol, (0, -1, 1, 2)[o], 4)

    def y_copies(d, i):
        o, band = PATHS[d][i]
        here, there = rows.at[band, part_of(block_of(o), d)], cols.at[band, part_of(block_of(o), d)]
        device = (south, north)[d]
        return here, there, device, ys.at[d, i], yr.at[d, i]

    def y_next(d, i):
        _, there, device, send, recv = y_copies(d, i)
        return remote(there, there, send, recv, device)

    def y_stay(d, i):
        here, there, _, _, _ = y_copies(d, i)
        return pltpu.make_async_copy(here, there, yl.at[d, i])

    def y_tick(tick):
        if tick < 8:
            @pl.when(offset == 0)
            def _():
                for d in range(2):
                    here, there, device, send, recv = y_copies(d, tick)
                    remote(here, there, send, recv, device).start()
                    y_stay(d, tick).start()

        for far in (1, 2):
            if 0 <= tick - far < 8:
                for d in range(2):
                    @pl.when(position[d] == far)
                    def _():
                        y_next(d, tick - far).wait_recv()
                        y_next(d, tick - far).start()

    def y_arrived(first, last):
        for i in range(first, last):
            for d in range(2):
                @pl.when(position[d] == 3)
                def _():
                    y_next(d, i).wait_recv()

                @pl.when(position[d] == 0)
                def _():
                    y_stay(d, i).wait()

    def x_start(h):
        x_copy(0, 0, h).start()
        x_copy(1, 1, h).start()
        x_copy(0, 1, h).start()
        x_copy(1, 0, h).start()

    def x_pass(h):
        for e in range(2):
            x_copy(e, e, h).wait_recv()
            x2_copy(e, h).start()

    chains = ((way, 4, 0, onward), (-way, 3, 4, backward))

    def toward(step, turn):
        return lax.rem(z + turn * step + 16, 8)

    def mate_copy(i):
        return remote(gram.at[i, 1 - core], mate.at[i], ms.at[i], mr.at[i], partner)

    def multiply(i):
        band, o = STREAMS[i]
        count = 2

        def product(h):
            def step(t, carry):
                at = pl.ds(pl.multiple_of(t * (8 // count), 8 // count), 8 // count)
                right = cols[band, pl.ds(part_of(block_of(o), 0), 2)].reshape(local, half)
                left = rows[band, at, h].reshape(8 // count * sub, half)
                value = lax.dot_general(left, right, (((1,), (1,)), ((), ())), preferred_element_type=jnp.float32)
                scale = rq[at, h, :, 2 * band : 2 * band + 1].reshape(8 // count * sub, 1)
                value = value * scale * cq[o, 2 * band : 2 * band + 1]
                value = jnp.round(value).astype(jnp.int32).astype(jnp.int16)
                gram[i, h, at] = value.reshape(8 // count, sub, local)
                return carry

            lax.fori_loop(0, count, step, 0)

        product(1 - core)
        mate_copy(i).start()
        product(core)

    def start(i):
        mate_copy(i).wait_recv()
        for c, (turn, length, first, device) in enumerate(chains):
            ring[i, 7 + c] = own(i, toward(length, turn)).astype(jnp.int16)
            remote(ring.at[i, 7 + c], ring.at[i, first], zs.at[i, first], zr.at[i, first], device).start()

    def z_arrived(i, k):
        remote(ring.at[i, k], ring.at[i, k], zs.at[i, k], zr.at[i, k], onward).wait_recv()

    def own(i, d):
        return gram[i, core, d].astype(jnp.int32) + mate[i, d].astype(jnp.int32)

    def advance(i, step):
        band, o = STREAMS[i]
        for turn, length, first, device in chains:
            if step < length:
                k = first + step
                z_arrived(i, k - 1)
                total = ring[i, k - 1].astype(jnp.int32) + own(i, toward(length - step, turn))
                ring[i, k - 1] = total.astype(jnp.int16)
                remote(ring.at[i, k - 1], ring.at[i, k], zs.at[i, k], zr.at[i, k], device).start()
        if step < 4:
            return
        z_arrived(i, 3)
        z_arrived(i, 6)
        final = ring[i, 3].astype(jnp.int32) + ring[i, 6].astype(jnp.int32) + own(i, z)
        final = final.astype(jnp.float32)
        final = final * rq[z, core, :, 2 * band + 1 : 2 * band + 2] * cq[o, 2 * band + 1 : 2 * band + 2]
        o_ref[band, :, pl.ds(pl.multiple_of(block_of(o) * local, local), local)] = final

    def frame_sums():
        wide = lax.broadcasted_iota(jnp.int32, (sub, 128), 1)
        for t in range(4):
            at = pl.ds(t * sub, sub)
            columns = jnp.zeros((sub, 128), jnp.float32)
            for band in range(2):
                plain = jnp.zeros((sub, 128), jnp.float32)
                square = jnp.zeros((sub, 128), jnp.float32)
                for r in range(4):
                    flat = s[band, r, at, :] * gain(band, r)
                    plain = plain + flat
                    square = square + flat * flat
                columns = jnp.where(wide == 2 * band, jnp.sum(plain, axis=1, keepdims=True), columns)
                columns = jnp.where(wide == 2 * band + 1, jnp.sum(square, axis=1, keepdims=True), columns)
            s[0, 0, at, :] = columns
        pc[core] = jnp.transpose(s[0, 0])[:8]

    def scales(total):
        result = []
        for band in range(2):
            norm = jnp.sqrt(total[2 * band + 1 : 2 * band + 2])
            result += [(SCALE**0.5) / norm, norm * (pixels / (SCALE * pixels) ** 0.5) / total[2 * band : 2 * band + 1]]
        return jnp.concatenate([*result, jnp.zeros((4, local), jnp.float32)], axis=0)

    partner_sums = exchange(pc, core, [partner], pcs, pcr)
    z_sums = exchange(pz, z, z_peers, pzs, pzr)
    x_sums = exchange(rsum, tcol, x_peers, rss, rsr)
    y_sums = [remote(rsum, csum, css.at[i], csr.at[i], peer) for i, peer in enumerate(y_peers)]

    def tick(t):
        if t == 0:
            flatten(0)
            x_start(0)
        if t in (1, 4):
            x_pass(t // 4)
        if t in (2, 5):
            for e in range(2):
                x_copy(1 - e, e, t // 4).wait_recv()
        if t in (3, 6):
            for e in range(2):
                x2_copy(e, t // 4).wait_recv()
        y_tick(t)
        if t == 0:
            frame_sums()
            partner_sums[0].start()
            flatten(1)
            partner_sums[0].wait_recv()
            pz[z] = add_up(pc, 2)
            for copy in z_sums:
                copy.start()
        if t == 1:
            for copy in z_sums:
                copy.wait_recv()
            rsum[tcol] = scales(add_up(pz, 8))
            for copy in x_sums:
                copy.start()
            x_start(1)
        if t == 2:
            for copy in x_sums:
                copy.wait_recv()

            @pl.when(offset == 0)
            def _():
                for copy in y_sums:
                    copy.start()

            for block in range(4):
                tall = jnp.transpose(jnp.concatenate([rsum[block], jnp.zeros((120, local), jnp.float32)], axis=0))
                rq[2 * block : 2 * block + 2] = tall.reshape(2, 2, sub, 128)

    def take_sums():
        for i in range(3):
            @pl.when(offset == i + 1)
            def _():
                y_sums[i].wait_recv()

        for o in range(4):
            cq[o] = jnp.where(offset == 0, rsum[block_of(o)], csum[block_of(o)])

    for run in plan(tick, take_sums, y_arrived, multiply, start, advance):
        run()

    for i in range(8):
        mate_copy(i).wait_send()
    for band in range(2):
        for e in range(2):
            x_copy(0, e, band).wait_send()
            x_copy(1, e, band).wait_send()
            x2_copy(e, band).wait_send()
    for d in range(2):
        @pl.when(position[d] < 3)
        def _():
            for i in range(8):
                y_next(d, i).wait_send()

    for copy in [*partner_sums, *z_sums, *x_sums]:
        copy.wait_send()

    @pl.when(offset == 0)
    def _():
        for copy in y_sums:
            copy.wait_send()

    def sent(step, carry):
        for i in range(8):
            remote(ring.at[i, step], ring.at[i, step], zs.at[i, step], zr.at[i, step], onward).wait_send()
        return carry

    lax.fori_loop(0, 7, sent, 0)


def per_device(frames, drift):
    local, _, tile_rows, columns = frames.shape
    total_frames = local * lax.axis_size("trow") * lax.axis_size("tcol")
    band_pixels = tile_rows * columns * lax.axis_size("pix")
    plain = frames.astype(jnp.bfloat16).transpose(1, 2, 0, 3)
    up = jnp.maximum(drift, 0).astype(jnp.float32) / 8.0
    down = jnp.maximum(-drift, 0).astype(jnp.float32) / 8.0
    stay = 1.0 - up - down
    weights = jnp.stack([stay[:, 0], up[:, 0], down[:, 0], stay[:, 1], up[:, 1], down[:, 1]], axis=1)

    dma = pltpu.SemaphoreType.DMA
    vmem = pl.BlockSpec(memory_space=pltpu.VMEM)
    block, half, sub = 4 * local, tile_rows * columns, local // 4
    f32, bf16, i16 = jnp.float32, jnp.bfloat16, jnp.int16
    out = pl.pallas_call(
        functools.partial(twotime_kernel, frames=float(total_frames), pixels=float(band_pixels)),
        out_shape=jax.ShapeDtypeStruct((2, block // 16, block), jnp.float32),
        in_specs=[vmem, vmem],
        out_specs=vmem,
        scratch_shapes=[
            pltpu.VMEM((2, 2, local, columns), bf16),
            pltpu.VMEM((2, tile_rows, local, columns), f32),
            pltpu.VMEM((2, 8, 2, sub, half), bf16),
            pltpu.VMEM((2, 8, 2, sub, half), bf16),
            pltpu.VMEM((8, 2, 8, sub, local), i16),
            pltpu.VMEM((8, 8, sub, local), i16),
            pltpu.VMEM((8, 9, sub, local), i16),
            pltpu.VMEM((4, 8, columns), f32),
            pltpu.VMEM((4, 8, columns), f32),
            pltpu.VMEM((2, 8, local), f32),
            pltpu.VMEM((8, 8, local), f32),
            pltpu.VMEM((4, 8, local), f32),
            pltpu.VMEM((4, 8, local), f32),
            pltpu.VMEM((8, 2, sub, 128), f32),
            pltpu.VMEM((4, 8, local), f32),
            dma((2,)), dma((2,)), dma((3,)), dma((3,)), dma((3,)), dma((3,)), dma((8,)), dma((8,)),
            dma((2, 2, 2)), dma((2, 2, 2)), dma((2, 2)), dma((2, 2)), dma((2, 8)), dma((2, 8)), dma((2, 8)),
            dma((1,)), dma((1,)), dma((7,)), dma((7,)), dma((3,)), dma((3,)), dma((3,)), dma((3,)),
            dma((8, 7)), dma((8, 7)),
        ],
        compiler_params=pltpu.CompilerParams(collective_id=0, has_side_effects=True, vmem_limit_bytes=48 << 20),
        name="twotime",
    )(plain, weights)
    return out[0], out[1]


def solution(mesh):
    in_specs = (P(("trow", "tcol"), None, "pix", None), P(("trow", "tcol"), None))
    out_specs = (P(("trow", "pix"), "tcol"), P(("trow", "pix"), "tcol"))
    return jax.shard_map(
        per_device, mesh=mesh, in_specs=in_specs, out_specs=out_specs, check_vma=False
    )
```

time: 127 us -> 106 us (0.83); the launches traced: 125 us -> 106 us
  Pallas kernels: 121 us -> 102 us
    pallas_call x1, Pallas kernels: 121 us -> 102 us  [per_device(): pl.pallas_call(functools.partial(twotime_kernel, frames=float(total_frame...]
where the time goes in v3:
time: 106 us
  Pallas kernels  102 us (96%)
  local copies, waits for them, and re-layouts  2.99 us (3%)
    pallas_call x1, Pallas kernels, per_device(): pl.pallas_call(functools.partial(twotime_kernel, frames=float(total_frame...  102 us

profile of v3, /device:TPU:8, one launch (start us, length us, event | category | flops | bytes accessed | tf_op | source)
XLA Modules:
  0.0 105.9 jit_solution(4308748756303888200)
XLA Ops:
  0.6 0.7 convert_multiply_fusion
  1.4 0.1 copy.8.w_ref
  1.5 1.7 %copy.12 = bf16[384,2,4,128]{3,0,2,1:T(8,128)(2,1)S(1)} copy(f32[384,2,4,128]{3,2,1,0:T(4,128)} %param.2) | data formatting | bytes 2359296 | tf_op args[0]
  3.2 101.5 %twotime.1 = f32[2,96,1536]{2,1,0:T(8,128)S(1)} custom-call(bf16[2,4,384,128]{3,2,1,0:T(8,128)(2,1)S(1)} %bitcast.7, f32[384,6]{1,0:T(8,128)S(1)} %copy.8.w_ref), custom_call_target="tpu_custom_call" | custom-call | tf_op jit(solution)/shard_map/twotime/pallas_call | solution.py:405
  104.8 1.1 %slice_bitcast_fusion = (f32[96,1536]{1,0:T(8,128)}, f32[96,1536]{1,0:T(8,128)}) fusion(f32[2,96,1536]{2,1,0:T(8,128)S(1)} %twotime.1), kind=kLoop, calls=%fused_computation.2 | loop fusion | bytes 2359296 | tf_op jit(solution)/shard_map/squeeze | solution.py:434
  (3 shorter events, 0.0 us)

commit v4 on v3

--- a/solution.py
+++ b/solution.py
@@ -28,7 +28,7 @@
 
 
 def plan(tick, take_sums, y_arrived, multiply, start, advance):
-    beat, hop, wire = 5.0, 2.5, 1.5
+    beat, hop, wire = 4.5, 3.0, 1.5
     todo = [(beat * t, 0, lambda t=t: tick(t)) for t in range(10)]
     ready = [beat * t for t in (4.4, 5.6, 5.7, 6.8, 7.6, 9.5, 9.6, 10.7)]
     clock, free, events = 0.0, 0.0, []
@@ -150,13 +150,13 @@
                     flat = s[band, r, at, :] * gain(band, r)
                     rows[band, part_of(tcol, e), h, :, r * 128 : (r + 1) * 128] = flat.astype(jnp.bfloat16)
 
-    def x_copy(d, e, band):
-        place = rows.at[band, part_of(tcol, e)]
-        return remote(place, place, xs.at[d, e, band], xr.at[d, e, band], (east, west)[d])
-
-    def x2_copy(e, band):
-        place = rows.at[band, part_of(around(tcol, (-1, 1)[e], 4), e)]
-        return remote(place, place, x2s.at[e, band], x2r.at[e, band], (east, west)[e])
+    def x_copy(d, e, band, h):
+        place = rows.at[band, part_of(tcol, e), h]
+        return remote(place, place, xs.at[d, e, band, h], xr.at[d, e, band, h], (east, west)[d])
+
+    def x2_copy(e, band, h):
+        place = rows.at[band, part_of(around(tcol, (-1, 1)[e], 4), e), h]
+        return remote(place, place, x2s.at[e, band, h], x2r.at[e, band, h], (east, west)[e])
 
     offset = around(trow, -tcol, 4)
     position = (offset, around(0, -offset, 4))
@@ -170,9 +170,9 @@
         device = (south, north)[d]
         return here, there, device, ys.at[d, i], yr.at[d, i]
 
-    def y_next(d, i):
+    def y_next(d, i, h):
         _, there, device, send, recv = y_copies(d, i)
-        return remote(there, there, send, recv, device)
+        return remote(there.at[h], there.at[h], send.at[h], recv.at[h], device)
 
     def y_stay(d, i):
         here, there, _, _, _ = y_copies(d, i)
@@ -182,40 +182,44 @@
         if tick < 8:
             @pl.when(offset == 0)
             def _():
+                for h in range(2):
+                    for d in range(2):
+                        here, there, device, send, recv = y_copies(d, tick)
+                        remote(here.at[h], there.at[h], send.at[h], recv.at[h], device).start()
                 for d in range(2):
-                    here, there, device, send, recv = y_copies(d, tick)
-                    remote(here, there, send, recv, device).start()
                     y_stay(d, tick).start()
 
         for far in (1, 2):
             if 0 <= tick - far < 8:
-                for d in range(2):
-                    @pl.when(position[d] == far)
-                    def _():
-                        y_next(d, tick - far).wait_recv()
-                        y_next(d, tick - far).start()
+                for h in range(2):
+                    for d in range(2):
+                        @pl.when(position[d] == far)
+                        def _():
+                            y_next(d, tick - far, h).wait_recv()
+                            y_next(d, tick - far, h).start()
 
     def y_arrived(first, last):
         for i in range(first, last):
             for d in range(2):
                 @pl.when(position[d] == 3)
                 def _():
-                    y_next(d, i).wait_recv()
+                    for h in range(2):
+                        y_next(d, i, h).wait_recv()
 
                 @pl.when(position[d] == 0)
                 def _():
                     y_stay(d, i).wait()
 
-    def x_start(h):
-        x_copy(0, 0, h).start()
-        x_copy(1, 1, h).start()
-        x_copy(0, 1, h).start()
-        x_copy(1, 0, h).start()
-
-    def x_pass(h):
-        for e in range(2):
-            x_copy(e, e, h).wait_recv()
-            x2_copy(e, h).start()
+    def x_start(band, step):
+        for h in range(2):
+            for d in range(2):
+                x_copy(d, (d + step) % 2, band, h).start()
+
+    def x_pass(band):
+        for h in range(2):
+            for e in range(2):
+                x_copy(e, e, band, h).wait_recv()
+                x2_copy(e, band, h).start()
 
     chains = ((way, 4, 0, onward), (-way, 3, 4, backward))
 
@@ -309,17 +313,22 @@
     def tick(t):
         if t == 0:
             flatten(0)
-            x_start(0)
+            x_start(0, 0)
         if t in (1, 4):
             x_pass(t // 4)
         if t in (2, 5):
             for e in range(2):
-                x_copy(1 - e, e, t // 4).wait_recv()
+                for h in range(2):
+                    x_copy(1 - e, e, t // 4, h).wait_recv()
         if t in (3, 6):
             for e in range(2):
-                x2_copy(e, t // 4).wait_recv()
+                for h in range(2):
+                    x2_copy(e, t // 4, h).wait_recv()
         y_tick(t)
+        if t in (2, 3):
+            x_start(1, t - 2)
         if t == 0:
+            x_start(0, 1)
             frame_sums()
             partner_sums[0].start()
             flatten(1)
@@ -333,8 +342,7 @@
             rsum[tcol] = scales(add_up(pz, 8))
             for copy in x_sums:
                 copy.start()
-            x_start(1)
-        if t == 2:
+        if t == 3:
             for copy in x_sums:
                 copy.wait_recv()
 
@@ -363,14 +371,16 @@
         mate_copy(i).wait_send()
     for band in range(2):
         for e in range(2):
-            x_copy(0, e, band).wait_send()
-            x_copy(1, e, band).wait_send()
-            x2_copy(e, band).wait_send()
+            for h in range(2):
+                x_copy(0, e, band, h).wait_send()
+                x_copy(1, e, band, h).wait_send()
+                x2_copy(e, band, h).wait_send()
     for d in range(2):
         @pl.when(position[d] < 3)
         def _():
             for i in range(8):
-                y_next(d, i).wait_send()
+                for h in range(2):
+                    y_next(d, i, h).wait_send()
 
     for copy in [*partner_sums, *z_sums, *x_sums]:
         copy.wait_send()
@@ -424,7 +434,7 @@
             pltpu.VMEM((8, 2, sub, 128), f32),
             pltpu.VMEM((4, 8, local), f32),
             dma((2,)), dma((2,)), dma((3,)), dma((3,)), dma((3,)), dma((3,)), dma((8,)), dma((8,)),
-            dma((2, 2, 2)), dma((2, 2, 2)), dma((2, 2)), dma((2, 2)), dma((2, 8)), dma((2, 8)), dma((2, 8)),
+            dma((2, 2, 2, 2)), dma((2, 2, 2, 2)), dma((2, 2, 2)), dma((2, 2, 2)), dma((2, 8, 2)), dma((2, 8, 2)), dma((2, 8)),
             dma((1,)), dma((1,)), dma((7,)), dma((7,)), dma((3,)), dma((3,)), dma((3,)), dma((3,)),
             dma((8, 7)), dma((8, 7)),
         ],

time: 106 us -> 105 us (level)
  Pallas kernels: 102 us -> 100 us
    pallas_call x1, Pallas kernels: 102 us -> 100 us  [per_device(): pl.pallas_call(functools.partial(twotime_kernel, frames=float(total_frame...]
where the time goes in v4:
time: 105 us
  Pallas kernels  100 us (95%)
  local copies, waits for them, and re-layouts  2.99 us (3%)
    pallas_call x1, Pallas kernels, per_device(): pl.pallas_call(functools.partial(twotime_kernel, frames=float(total_frame...  100 us

profile of v4, /device:TPU:8, one launch (start us, length us, event | category | flops | bytes accessed | tf_op | source)
XLA Modules:
  0.0 104.8 jit_solution(14971971753375019372)
XLA Ops:
  0.6 0.7 convert_multiply_fusion
  1.4 0.1 copy.8.w_ref
  1.5 1.7 %copy.12 = bf16[384,2,4,128]{3,0,2,1:T(8,128)(2,1)S(1)} copy(f32[384,2,4,128]{3,2,1,0:T(4,128)} %param.2) | data formatting | bytes 2359296 | tf_op args[0]
  3.2 100.4 %twotime.1 = f32[2,96,1536]{2,1,0:T(8,128)S(1)} custom-call(bf16[2,4,384,128]{3,2,1,0:T(8,128)(2,1)S(1)} %bitcast.7, f32[384,6]{1,0:T(8,128)S(1)} %copy.8.w_ref), custom_call_target="tpu_custom_call" | custom-call | tf_op jit(solution)/shard_map/twotime/pallas_call | solution.py:415
  103.7 1.1 %slice_bitcast_fusion = (f32[96,1536]{1,0:T(8,128)}, f32[96,1536]{1,0:T(8,128)}) fusion(f32[2,96,1536]{2,1,0:T(8,128)S(1)} %twotime.1), kind=kLoop, calls=%fused_computation.2 | loop fusion | bytes 2359296 | tf_op jit(solution)/shard_map/squeeze | solution.py:444
  (3 shorter events, 0.0 us)

commit v5 on v4

--- a/solution.py
+++ b/solution.py
@@ -58,7 +58,7 @@
 def twotime_kernel(
     x_ref, w_ref, o_ref,
     halo, s, rows, cols, gram, mate, ring, px, py, pc, pz, rsum, csum, rq, cq,
-    hs, hr, pxs, pxr, pys, pyr, ms, mr, xs, xr, x2s, x2r, ys, yr, yl,
+    hs, hr, pxs, pxr, pys, pyr, ms, mr, xs, xr, x2s, x2r, ys, yr, yl, yd,
     pcs, pcr, pzs, pzr, rss, rsr, css, csr, zs, zr,
     *, frames, pixels,
 ):
@@ -178,6 +178,10 @@
         here, there, _, _, _ = y_copies(d, i)
         return pltpu.make_async_copy(here, there, yl.at[d, i])
 
+    def y_direct(d, h):
+        here, there, _, _, recv = y_copies(d, 7)
+        return remote(here.at[h], there.at[h], yd.at[d, h], recv.at[h], (north, south)[d])
+
     def y_tick(tick):
         if tick < 8:
             @pl.when(offset == 0)
@@ -188,6 +192,10 @@
                         remote(here.at[h], there.at[h], send.at[h], recv.at[h], device).start()
                 for d in range(2):
                     y_stay(d, tick).start()
+                if tick == 7:
+                    for d in range(2):
+                        for h in range(2):
+                            y_direct(d, h).start()
 
         for far in (1, 2):
             if 0 <= tick - far < 8:
@@ -196,7 +204,8 @@
                         @pl.when(position[d] == far)
                         def _():
                             y_next(d, tick - far, h).wait_recv()
-                            y_next(d, tick - far, h).start()
+                            if (far, tick) != (2, 9):
+                                y_next(d, tick - far, h).start()
 
     def y_arrived(first, last):
         for i in range(first, last):
@@ -378,9 +387,19 @@
     for d in range(2):
         @pl.when(position[d] < 3)
         def _():
-            for i in range(8):
+            for i in range(7):
                 for h in range(2):
                     y_next(d, i, h).wait_send()
+
+        @pl.when(position[d] < 2)
+        def _():
+            for h in range(2):
+                y_next(d, 7, h).wait_send()
+
+        @pl.when(offset == 0)
+        def _():
+            for h in range(2):
+                y_direct(d, h).wait_send()
 
     for copy in [*partner_sums, *z_sums, *x_sums]:
         copy.wait_send()
@@ -434,7 +453,7 @@
             pltpu.VMEM((8, 2, sub, 128), f32),
             pltpu.VMEM((4, 8, local), f32),
             dma((2,)), dma((2,)), dma((3,)), dma((3,)), dma((3,)), dma((3,)), dma((8,)), dma((8,)),
-            dma((2, 2, 2, 2)), dma((2, 2, 2, 2)), dma((2, 2, 2)), dma((2, 2, 2)), dma((2, 8, 2)), dma((2, 8, 2)), dma((2, 8)),
+            dma((2, 2, 2, 2)), dma((2, 2, 2, 2)), dma((2, 2, 2)), dma((2, 2, 2)), dma((2, 8, 2)), dma((2, 8, 2)), dma((2, 8)), dma((2, 2)),
             dma((1,)), dma((1,)), dma((7,)), dma((7,)), dma((3,)), dma((3,)), dma((3,)), dma((3,)),
             dma((8, 7)), dma((8, 7)),
         ],

time: 105 us -> 105 us (level)
  no operation moved by 1% of the time
where the time goes in v5:
time: 105 us
  Pallas kernels  100 us (95%)
  local copies, waits for them, and re-layouts  2.99 us (3%)
    pallas_call x1, Pallas kernels, per_device(): pl.pallas_call(functools.partial(twotime_kernel, frames=float(total_frame...  100 us

profile of v5, /device:TPU:8, one launch (start us, length us, event | category | flops | bytes accessed | tf_op | source)
XLA Modules:
  0.0 104.8 jit_solution(8540793913542348774)
XLA Ops:
  0.6 0.7 convert_multiply_fusion
  1.4 0.1 copy.8.w_ref
  1.5 1.7 %copy.12 = bf16[384,2,4,128]{3,0,2,1:T(8,128)(2,1)S(1)} copy(f32[384,2,4,128]{3,2,1,0:T(4,128)} %param.2) | data formatting | bytes 2359296 | tf_op args[0]
  3.2 100.5 %twotime.1 = f32[2,96,1536]{2,1,0:T(8,128)S(1)} custom-call(bf16[2,4,384,128]{3,2,1,0:T(8,128)(2,1)S(1)} %bitcast.7, f32[384,6]{1,0:T(8,128)S(1)} %copy.8.w_ref), custom_call_target="tpu_custom_call" | custom-call | tf_op jit(solution)/shard_map/twotime/pallas_call | solution.py:434
  103.7 1.1 %slice_bitcast_fusion = (f32[96,1536]{1,0:T(8,128)}, f32[96,1536]{1,0:T(8,128)}) fusion(f32[2,96,1536]{2,1,0:T(8,128)S(1)} %twotime.1), kind=kLoop, calls=%fused_computation.2 | loop fusion | bytes 2359296 | tf_op jit(solution)/shard_map/squeeze | solution.py:463
  (3 shorter events, 0.0 us)

commit v6 on v5

--- a/solution.py
+++ b/solution.py
@@ -240,7 +240,7 @@
 
     def multiply(i):
         band, o = STREAMS[i]
-        count = 2
+        count = 1
 
         def product(h):
             def step(t, carry):

time: 105 us -> 104 us (level)
  no operation moved by 1% of the time
where the time goes in v6:
time: 104 us
  Pallas kernels  99.8 us (96%)
  local copies, waits for them, and re-layouts  2.99 us (3%)
    pallas_call x1, Pallas kernels, per_device(): pl.pallas_call(functools.partial(twotime_kernel, frames=float(total_frame...  99.8 us

profile of v6, /device:TPU:8, one launch (start us, length us, event | category | flops | bytes accessed | tf_op | source)
XLA Modules:
  0.0 104.1 jit_solution(4575826834241224716)
XLA Ops:
  0.6 0.7 convert_multiply_fusion
  1.4 0.1 copy.8.w_ref
  1.5 1.7 %copy.12 = bf16[384,2,4,128]{3,0,2,1:T(8,128)(2,1)S(1)} copy(f32[384,2,4,128]{3,2,1,0:T(4,128)} %param.2) | data formatting | bytes 2359296 | tf_op args[0]
  3.2 99.8 %twotime.1 = f32[2,96,1536]{2,1,0:T(8,128)S(1)} custom-call(bf16[2,4,384,128]{3,2,1,0:T(8,128)(2,1)S(1)} %bitcast.7, f32[384,6]{1,0:T(8,128)S(1)} %copy.8.w_ref), custom_call_target="tpu_custom_call" | custom-call | tf_op jit(solution)/shard_map/twotime/pallas_call | solution.py:434
  103.0 1.1 %slice_bitcast_fusion = (f32[96,1536]{1,0:T(8,128)}, f32[96,1536]{1,0:T(8,128)}) fusion(f32[2,96,1536]{2,1,0:T(8,128)S(1)} %twotime.1), kind=kLoop, calls=%fused_computation.2 | loop fusion | bytes 2359296 | tf_op jit(solution)/shard_map/squeeze | solution.py:463
  (3 shorter events, 0.0 us)
